TPU v7x, 128 devices: a whole 4x4x4 slice. The times are simulated.
128 devices in a mesh: song: 2 (over y_lo), seq: 64 (over z, x, y_hi, core).
Axes of the slice: x: 4, y: 4 (y_hi: 2, y_lo: 2; y = y_hi * 2 + y_lo), z: 4, core: 2. Of those that a mesh axis runs over, the one named last changes fastest.
Arguments:
- song_ids: int32 [16384], P(('song', 'seq')), parts along dimension 0, may hold values from 0 to 2047
- table: bfloat16 [2048, 2432], P(None, 'seq'), may hold values from -6 to 6
- position_table: bfloat16 [8192, 2432], P('seq'), may hold values from -4 to 4
- w_qkv: bfloat16 [2, 2432, 1800], replicated, may hold values from -4 to 4
- w_out: bfloat16 [2, 600, 2432], replicated, may hold values from -0.25 to 0.25
Outputs:
- stream_out: bfloat16 [16384, 2432], P(('song', 'seq')), parts along dimension 0
There are 2 independent parts, one for each index of `song`. A program takes and returns all parts, laid end to end along the dimension named above; an argument that names none is the same for every part. Nothing has to cross between parts.
All inputs are finite; a program needn't handle non-finite values.
Results may differ from a plain program's by a relative error of at most 0.0065.
Values may be sent and summed in bfloat16 or wider, within the bound.
No kernel may reach another device: no remote copies, remote signals or barrier semaphores. Data moves between devices by JAX's collectives and lax.ppermute only.
A program may use at most 192 MiB of HBM per device.

v0:
```python
import math
import jax
import jax.numpy as jnp
from jax import lax
from jax.sharding import PartitionSpec as P

HEADS = 4
HEAD = 150
epsilon = 1e-05


def from_behind(value, axis, by):
    length = lax.axis_size(axis)
    pairs = [(i, i + by) for i in range(length) if 0 <= i + by < length]
    return lax.ppermute(value, axis, pairs)


def normalize(residual):
    center_mean = jnp.mean(residual, axis=-1, keepdims=True)
    centered = residual - center_mean
    variance = jnp.mean(centered * centered, axis=-1, keepdims=True)
    return (centered * lax.rsqrt(variance + epsilon)).astype(jnp.bfloat16)


def project(residual, weight):
    joined = jnp.dot(normalize(residual), weight, preferred_element_type=jnp.float32).astype(
        jnp.bfloat16
    )
    return joined.reshape(residual.shape[0], HEADS, 3 * HEAD)


def softmax_rounded(scores):
    top_score = jnp.max(scores, axis=-1, keepdims=True)
    lifted = jnp.exp(scores - top_score)
    return (lifted / jnp.sum(lifted, axis=-1, keepdims=True)).astype(jnp.bfloat16)


def shards(song_ids, table, position_table, w_qkv, w_out):
    inv_root = 1.0 / math.sqrt(HEAD)
    axis_count = lax.axis_size("seq")
    row_index = lax.axis_index("seq")
    all_codes = lax.all_gather(song_ids, "seq", axis=0, tiled=True)
    picked = jnp.take(table, all_codes, axis=0)
    embedded = lax.all_to_all(picked, "seq", split_axis=0, concat_axis=1, tiled=True)
    residual = embedded.astype(jnp.float32) + position_table.astype(jnp.float32)
    local_tokens = residual.shape[0]
    joined = project(residual, w_qkv[0])
    every_row = lax.all_gather(joined[:, :, HEAD:], "seq", axis=0, tiled=True)
    row_grid = every_row.reshape(axis_count, local_tokens, HEADS, 2 * HEAD)
    scores = (
        jnp.einsum(
            "chd,rchd->chr",
            joined[:, :, :HEAD],
            row_grid[..., :HEAD],
            preferred_element_type=jnp.float32,
        )
        * inv_root
    )
    allowed = jnp.arange(axis_count) <= row_index
    probs = softmax_rounded(jnp.where(allowed, scores, -jnp.inf))
    mixed = jnp.einsum(
        "chr,rchd->chd", probs, row_grid[..., HEAD:], preferred_element_type=jnp.float32
    ).astype(jnp.bfloat16)
    residual = residual + jnp.dot(
        mixed.reshape(local_tokens, HEADS * HEAD), w_out[0], preferred_element_type=jnp.float32
    )
    joined = project(residual, w_qkv[1])
    before = from_behind(joined[:, :, HEAD:], "seq", 1)
    query = joined[:, :, :HEAD]
    far_scores = (
        jnp.einsum("chd,khd->hck", query, before[..., :HEAD], preferred_element_type=jnp.float32)
        * inv_root
    )
    far_scores = jnp.where(row_index > 0, far_scores, -jnp.inf)
    own_scores = (
        jnp.einsum(
            "chd,chd->hc", query, joined[:, :, HEAD : 2 * HEAD], preferred_element_type=jnp.float32
        )
        * inv_root
    )
    top_score = jnp.maximum(jnp.max(far_scores, axis=-1), own_scores)
    far_lifted = jnp.exp(far_scores - top_score[..., None])
    own_lifted = jnp.exp(own_scores - top_score)
    total = jnp.sum(far_lifted, axis=-1) + own_lifted
    far_probs = (far_lifted / total[..., None]).astype(jnp.bfloat16)
    own_probs = (own_lifted / total).astype(jnp.bfloat16)
    far_part = jnp.einsum(
        "hck,khd->chd", far_probs, before[..., HEAD:], preferred_element_type=jnp.float32
    )
    own_part = jnp.transpose(own_probs.astype(jnp.float32))[..., None] * joined[
        :, :, 2 * HEAD :
    ].astype(jnp.float32)
    mixed = (far_part + own_part).astype(jnp.bfloat16)
    residual = residual + jnp.dot(
        mixed.reshape(local_tokens, HEADS * HEAD), w_out[1], preferred_element_type=jnp.float32
    )
    return residual.astype(jnp.bfloat16)


def solution(mesh):
    in_specs = (P(("song", "seq")), P(None, "seq"), P("seq", None), P(), P())
    out_specs = P(("song", "seq"), None)
    return jax.shard_map(shards, mesh=mesh, in_specs=in_specs, out_specs=out_specs, check_vma=False)
```

profile of v0, /device:TPU:32, one launch (start us, length us, event | category | flops | bytes accessed | tf_op | source)
XLA Modules:
  0.0 349.5 jit_solution(981527527557596328)
XLA Ops:
  6.5 0.0 all-gather.3.cloned.1.call-start
  6.5 83.1 %all-gather = s32[64,1,128]{2,1,0:T(1,128)S(1)} all-gather(s32[1,1,128]{2,1,0:T(1,128)} %bitcast.80), channel_id=1, replica_groups=mesh['song'=2,'seq'=64] {'seq'}, dimensions={0}, use_global_device_ids=true | all-gather | bytes 33280 | tf_op jit(solution)/shard_map/all_gather | solution.py:42
  89.7 1.2 copy.17
  90.9 24.0 %gather_fusion = bf16[8192,38]{1,0:T(8,128)(2,1)S(1)} fusion(bf16[2048,38]{1,0:T(8,128)(2,1)S(1)} %copy.17, s32[8192]{0:T(1024)S(1)} %fusion.43), kind=kCustom, calls=%fused_computation | custom fusion | bytes 1277952 | tf_op jit(solution)/shard_map/jit(_take)/gather | solution.py:43
  115.0 1.0 copy.18
  116.0 0.1 broadcast_select_fusion
  116.1 31.4 %all_to_all.10 = bf16[64,128,38]{1,2,0:T(8,128)(2,1)S(1)} all-to-all(bf16[64,128,38]{1,2,0:T(8,128)(2,1)S(1)} %broadcast_select_fusion), channel_id=1, replica_groups=mesh['song'=2,'seq'=64] {'seq'}, dimensions={0} | all-to-all | bytes 1245184 | tf_op jit(solution)/shard_map/all_to_all | solution.py:44
  147.5 0.1 convert_bitcast_fusion
  147.6 0.1 reshape.65
  147.7 0.0 copy-start
  147.7 0.4 copy.19
  148.1 0.7 copy-done
  148.7 0.2 fusion.39
  149.0 0.3 multiply_reduce_fusion.3
  149.3 6.2 %fusion.13 = bf16[128,1800]{0,1:T(8,128)(2,1)S(1)} fusion(bf16[2,2432,1800]{1,2,0:T(8,128)(2,1)} %param.8, f32[128]{0:T(128)S(1)} %add_rsqrt_fusion.1, f32[128]{0:T(128)S(1)} %broadcast_multiply_fusion.1, f32[128,2432]{1,0:T(8,128)S(1)} %copy.19, bf16[128,2432]{1,0:T(8,128)(2,1)S(1)} %copy-done), kind=kOutput, calls=%fused_computation.20 | convolution fusion | flops 1122452480 | bytes 11084800 | tf_op jit(solution)/shard_map/dot_general | solution.py:26
  155.5 0.1 reshape.60
  155.6 0.8 slice.59
  156.4 0.0 all-gather.3.cloned.1.call-update
  156.5 117.3 %all-gather.3.cloned.1.call-done = bf16[8192,4,300]{0,2,1:T(8,128)(2,1)} async-done(((bf16[128,4,300]{0,2,1:T(8,128)(2,1)}), bf16[8192,4,300]{0,2,1:T(8,128)(2,1)}) %all-gather.3.cloned.1.call-update) | async-done | bytes 19660816 | tf_op jit(solution)/shard_map/all_gather | solution.py:48
  273.8 27.6 %reshape.61 = bf16[64,128,4,300]{1,0,3,2:T(8,128)(2,1)} reshape(bf16[8192,4,300]{0,2,1:T(8,128)(2,1)} %all-gather.3.cloned.1.call-done) | data formatting | bytes 39321600 | tf_op jit(solution)/shard_map/reshape | solution.py:49
  301.3 6.7 %multiply_reduce_fusion.1 = f32[128,4,64]{0,2,1:T(8,128)S(1)} fusion(bf16[64,128,4,300]{1,0,3,2:T(8,128)(2,1)} %reshape.61, f32[128,4,150]{0,2,1:T(8,128)S(1)} %slice_convert_fusion), kind=kLoop, calls=%fused_computation.4 | loop fusion | flops 14712832 | bytes 10268672 | tf_op jit(solution)/shard_map/chd,rchd->chr/dot_general | solution.py:51
  308.0 0.1 fusion.26
  308.2 8.3 %multiply_reduce_fusion = bf16[128,4,150]{0,2,1:T(8,128)(2,1)S(1)} fusion(bf16[64,128,4,300]{1,0,3,2:T(8,128)(2,1)} %reshape.61, f32[128,4,64]{0,2,1:T(8,128)S(1)} %fusion.26), kind=kLoop, calls=%fused_computation.3 | loop fusion | flops 14668800 | bytes 10115072 | tf_op jit(solution)/shard_map/chr,rchd->chd/dot_general | solution.py:61
  316.6 2.6 fusion.53
  319.2 0.3 multiply_reduce_fusion.2
  319.5 6.2 %fusion.16 = bf16[128,1800]{0,1:T(8,128)(2,1)S(1)} fusion(bf16[2,2432,1800]{1,2,0:T(8,128)(2,1)} %param.8, f32[128,2432]{1,0:T(8,128)S(1)} %get-tuple-element.6, f32[128]{0:T(128)S(1)} %add_rsqrt_fusion, f32[128]{0:T(128)S(1)} %broadcast_multiply_fusion), kind=kOutput, calls=%fused_computation.21 | convolution fusion | flops 1121829888 | bytes 10462208 | tf_op jit(solution)/shard_map/dot_general | solution.py:26
  325.7 0.1 reshape.63
  325.8 0.1 slice.62
  325.9 2.2 collective-permute-start
  328.1 0.1 fusion.31
  328.1 10.5 %collective-permute-done = bf16[128,4,300]{0,2,1:T(8,128)(2,1)S(1)} collective-permute-done((bf16[128,4,300]{0,2,1:T(8,128)(2,1)S(1)}, bf16[128,4,300]{0,2,1:T(8,128)(2,1)S(1)}, u32[]{:S(2)}, u32[]{:S(2)}) %collective-permute-start) | collective-permute-done | bytes 307232 | tf_op jit(solution)/shard_map/ppermute | solution.py:15
  338.6 0.3 fusion.54
  338.9 0.1 fusion.32
  339.0 0.3 fusion.21
  339.3 3.4 fusion.8
  (13 shorter events, 0.2 us)
Async XLA Ops:
  6.5 267.2 %all-gather.3.cloned.1.call-start = ((), (), s32[]{:S(2)}) async-start(), calls=%async_computation.1 | async-start | bytes 20234240 | tf_op jit(solution)/shard_map/all_gather | solution.py:48
  147.7 1.1 copy-start
  325.9 12.7 %collective-permute-start = (bf16[128,4,300]{0,2,1:T(8,128)(2,1)S(1)}, bf16[128,4,300]{0,2,1:T(8,128)(2,1)S(1)}, u32[]{:S(2)}, u32[]{:S(2)}) collective-permute-start(bf16[128,4,300]{0,2,1:T(8,128)(2,1)S(1)} %slice.62), channel_id=1, source_target_pairs={{0,1},{1,2},{2,3},{3,4},{4,5},{5,6},{6,7},{7,8},{8,9},{9,10},{10,1... | collective-permute-start | bytes 921608 | tf_op jit(solution)/shard_map/ppermute | solution.py:15
Sparse Core Ops, SparseCore 0:
  156.5 117.1 all-gather.2
where the time goes:
time: 350 us
  waiting for transfers between devices  128 us (37%)
  blocking collectives  115 us (33%)
  local copies, waits for them, and re-layouts  56.2 us (16%)
  matrix products  18.9 us (5%)
  other arithmetic  16.4 us (5%)
  between operations  13.6 us (4%)
    all_gather x1, waiting for transfers between devices, shards(): every_row = lax.all_gather(joined[:, :, HEAD:], 'seq', axis=0, tiled=True)  117 us
    all_gather x1, blocking collectives, shards(): all_codes = lax.all_gather(song_ids, 'seq', axis=0, tiled=True)  83.1 us
    all_to_all x1, blocking collectives, shards(): lax.all_to_all(picked, 'seq', split_axis=0, concat_axis=1, tiled=True)  31.4 us
    reshape x1, local copies, waits for them, and re-layouts, shards(): row_grid = every_row.reshape(axis_count, local_tokens, HEADS, 2 * HEAD)  27.6 us
    gather x2, local copies, waits for them, and re-layouts, shards(): picked = jnp.take(table, all_codes, axis=0)  25 us
    dot_general x2, matrix products, project(): jnp.dot(normalize(residual), weight, preferred_element_type=jnp.float32)  12.3 us
    ppermute x1, waiting for transfers between devices, from_behind(): return lax.ppermute(value, axis, pairs)  10.5 us
    dot_general x1, other arithmetic, shards(): jnp.einsum('chr,rchd->chd', probs, row_grid[..., HEAD:], preferred_elemen...  8.34 us
  transfers between devices with their start and end apart: 2, of which 2 were waited for; matrix products, arithmetic and copies ran while one was open for 0% of the time, Pallas kernels for 0%

commit v1 on v0

--- a/solution.py
+++ b/solution.py
@@ -45,7 +45,16 @@
     residual = embedded.astype(jnp.float32) + position_table.astype(jnp.float32)
     local_tokens = residual.shape[0]
     joined = project(residual, w_qkv[0])
-    every_row = lax.all_gather(joined[:, :, HEAD:], "seq", axis=0, tiled=True)
+    arr = joined[:, :, HEAD:]
+    every_row = jnp.concatenate(
+        jax.lax.all_to_all(
+            jnp.stack([arr] * jax.lax.axis_size("seq"), axis=0),
+            axis_name="seq",
+            split_axis=0,
+            concat_axis=0,
+        ),
+        0,
+    )
     row_grid = every_row.reshape(axis_count, local_tokens, HEADS, 2 * HEAD)
     scores = (
         jnp.einsum(

time: 350 us -> 501 us (1.43); the launches traced: 350 us -> 494 us
  waiting for transfers between devices: 128 us -> 293 us
  local copies, waits for them, and re-layouts: 56.2 us -> 39.2 us
  between operations: 13.6 us -> 0.22 us
  starting transfers between devices: 2.17 us -> 9.1 us
    all_to_all x0 -> x1, waiting for transfers between devices: none -> 282 us  [shards(): jax.lax.all_to_all(jnp.stack([arr] * jax.lax.axis_size('seq'), axis=0), a...]
    all_gather x1 -> x0, waiting for transfers between devices: 117 us -> none  [shards(): every_row = lax.all_gather(joined[:, :, HEAD:], 'seq', axis=0, tiled=True)]
    reshape x1 -> x0, local copies, waits for them, and re-layouts: 27.6 us -> none  [shards(): row_grid = every_row.reshape(axis_count, local_tokens, HEADS, 2 * HEAD)]
    unnamed x1 -> x3, other arithmetic: 0.02 us -> 18.1 us
    dot_general x2 -> x0, other arithmetic: 15 us -> none  [the longest x1 8.34 us: shards(): jnp.einsum('chr,rchd->chd', probs, row_grid[..., HEAD:], preferred_elemen...]
    another operation x0 -> x1, local copies, waits for them, and re-layouts: none -> 10.9 us  [shards(): jnp.stack([arr] * jax.lax.axis_size('seq'), axis=0)]
    all_to_all x0 -> x1, starting transfers between devices: none -> 7.18 us  [shards(): jax.lax.all_to_all(jnp.stack([arr] * jax.lax.axis_size('seq'), axis=0), a...]
where the time goes in v1:
time: 501 us; the launch traced here: 494 us
  waiting for transfers between devices  293 us (58%)
  blocking collectives  115 us (23%)
  local copies, waits for them, and re-layouts  39.2 us (8%)
  other arithmetic  19.5 us (4%)
  matrix products  19.1 us (4%)
  starting transfers between devices  9.1 us (2%)
    all_to_all x1, waiting for transfers between devices, shards(): jax.lax.all_to_all(jnp.stack([arr] * jax.lax.axis_size('seq'), axis=0), a...  282 us
    all_gather x1, blocking collectives, shards(): all_codes = lax.all_gather(song_ids, 'seq', axis=0, tiled=True)  83.1 us
    all_to_all x1, blocking collectives, shards(): lax.all_to_all(picked, 'seq', split_axis=0, concat_axis=1, tiled=True)  31.4 us
    gather x2, local copies, waits for them, and re-layouts, shards(): picked = jnp.take(table, all_codes, axis=0)  25 us
    unnamed x3, other arithmetic  18.1 us
    dot_general x2, matrix products, project(): jnp.dot(normalize(residual), weight, preferred_element_type=jnp.float32)  12.3 us
    another operation x1, local copies, waits for them, and re-layouts, shards(): jnp.stack([arr] * jax.lax.axis_size('seq'), axis=0)  10.9 us
    ppermute x1, waiting for transfers between devices, from_behind(): return lax.ppermute(value, axis, pairs)  10.7 us
  transfers between devices with their start and end apart: 2, of which 2 were waited for; matrix products, arithmetic and copies ran while one was open for 0% of the time, Pallas kernels for 0%

profile of v1, /device:TPU:32, one launch (start us, length us, event | category | flops | bytes accessed | tf_op | source)
XLA Modules:
  0.0 494.2 jit_solution(4828239279460298627)
XLA Ops:
  0.0 83.1 %all-gather = s32[64,1,128]{2,1,0:T(1,128)S(1)} all-gather(s32[1,1,128]{2,1,0:T(1,128)} %bitcast.78), channel_id=1, replica_groups=mesh['song'=2,'seq'=64] {'seq'}, dimensions={0}, use_global_device_ids=true | all-gather | bytes 33280 | tf_op jit(solution)/shard_map/all_gather | solution.py:42
  83.2 1.2 copy.20
  84.4 24.0 %gather_fusion = bf16[8192,38]{1,0:T(8,128)(2,1)S(1)} fusion(bf16[2048,38]{1,0:T(8,128)(2,1)S(1)} %copy.20, s32[8192]{0:T(1024)S(1)} %fusion.45), kind=kCustom, calls=%fused_computation | custom fusion | bytes 1277952 | tf_op jit(solution)/shard_map/jit(_take)/gather | solution.py:43
  108.4 1.0 copy.21
  109.5 0.1 broadcast_select_fusion
  109.6 31.4 %all_to_all.15 = bf16[64,128,38]{1,2,0:T(8,128)(2,1)S(1)} all-to-all(bf16[64,128,38]{1,2,0:T(8,128)(2,1)S(1)} %broadcast_select_fusion), channel_id=1, replica_groups=mesh['song'=2,'seq'=64] {'seq'}, dimensions={0} | all-to-all | bytes 1245184 | tf_op jit(solution)/shard_map/all_to_all | solution.py:44
  140.9 0.1 convert_bitcast_fusion
  141.0 0.1 reshape.63
  141.1 0.0 copy-start
  141.1 0.4 copy.22
  141.5 0.7 copy-done
  142.2 0.2 fusion.41
  142.4 0.3 multiply_reduce_fusion.3
  142.7 6.2 %fusion.13 = bf16[128,1800]{0,1:T(8,128)(2,1)S(1)} fusion(bf16[2,2432,1800]{1,2,0:T(8,128)(2,1)} %param.8, f32[128]{0:T(128)S(1)} %add_rsqrt_fusion.1, f32[128]{0:T(128)S(1)} %broadcast_multiply_fusion.1, f32[128,2432]{1,0:T(8,128)S(1)} %copy.22, bf16[128,2432]{1,0:T(8,128)(2,1)S(1)} %copy-done), kind=kOutput, calls=%fused_computation.20 | convolution fusion | flops 1122452480 | bytes 11084800 | tf_op jit(solution)/shard_map/dot_general | solution.py:26
  148.9 0.1 reshape.59
  149.1 0.1 slice.59
  149.2 0.1 copy.23
  149.3 10.9 %stack.2 = bf16[64,128,4,300]{1,2,3,0:T(4,128)(2,1)} broadcast(bf16[128,4,300]{0,1,2:T(4,128)(2,1)S(1)} %copy.23), dimensions={1,2,3} | broadcast | bytes 19968000 | tf_op jit(solution)/shard_map/stack | solution.py:51
  160.2 7.2 %all-to-all-start.1 = ((bf16[64,128,4,300]{1,2,3,0:T(4,128)(2,1)}), bf16[64,128,4,300]{1,2,3,0:T(4,128)(2,1)}, u32[]{:S(2)}, u32[]{:S(2)}) async-start(bf16[64,128,4,300]{1,2,3,0:T(4,128)(2,1)} %stack.2), calls=%async_computation.1 | async-start | bytes 39321600 | tf_op jit(solution)/shard_map/all_to_all | solution.py:50
  167.4 0.1 copy.47
  167.5 281.9 %all-to-all-done.1 = bf16[64,128,4,300]{1,2,3,0:T(4,128)(2,1)} async-done(((bf16[64,128,4,300]{1,2,3,0:T(4,128)(2,1)}), bf16[64,128,4,300]{1,2,3,0:T(4,128)(2,1)}, u32[]{:S(2)}, u32[]{:S(2)}) %all-to-all-start.1) | async-done | bytes 19660832 | tf_op jit(solution)/shard_map/all_to_all | solution.py:50
  449.5 9.0 %multiply_reduce_fusion.1 = f32[128,4,64]{0,1,2:T(4,128)S(1)} fusion(bf16[64,128,4,300]{1,2,3,0:T(4,128)(2,1)} %all-to-all-done.1, f32[128,4,150]{0,1,2:T(4,128)S(1)} %copy.47), kind=kLoop, calls=%fused_computation.4 | loop fusion | flops 14712832 | bytes 10268672
  458.5 0.1 fusion.26
  458.6 0.1 copy.48
  458.7 9.1 %multiply_reduce_fusion = bf16[128,4,150]{0,1,2:T(4,128)(2,1)S(1)} fusion(bf16[64,128,4,300]{1,2,3,0:T(4,128)(2,1)} %all-to-all-done.1, f32[128,4,64]{0,1,2:T(4,128)S(1)} %copy.48), kind=kLoop, calls=%fused_computation.3 | loop fusion | flops 14668800 | bytes 10115072
  467.9 2.8 fusion.57
  470.7 0.3 multiply_reduce_fusion.2
  471.0 6.2 %fusion.16 = bf16[128,1800]{0,1:T(8,128)(2,1)S(1)} fusion(bf16[2,2432,1800]{1,2,0:T(8,128)(2,1)} %param.8, f32[128,2432]{1,0:T(8,128)S(1)} %get-tuple-element.6, f32[128]{0:T(128)S(1)} %add_rsqrt_fusion, f32[128]{0:T(128)S(1)} %broadcast_multiply_fusion), kind=kOutput, calls=%fused_computation.21 | convolution fusion | flops 1121829888 | bytes 10462208 | tf_op jit(solution)/shard_map/dot_general | solution.py:26
  477.2 0.1 reshape.61
  477.3 0.1 slice.62
  477.4 1.9 collective-permute-start
  479.3 0.1 fusion.31
  479.4 10.7 %collective-permute-done = bf16[128,4,300]{0,2,1:T(8,128)(2,1)S(1)} collective-permute-done((bf16[128,4,300]{0,2,1:T(8,128)(2,1)S(1)}, bf16[128,4,300]{0,2,1:T(8,128)(2,1)S(1)}, u32[]{:S(2)}, u32[]{:S(2)}) %collective-permute-start) | collective-permute-done | bytes 307232 | tf_op jit(solution)/shard_map/ppermute | solution.py:15
  490.1 0.3 fusion.58
  490.4 0.1 fusion.32
  490.5 0.3 fusion.21
  490.9 3.4 fusion.8
  (14 shorter events, 0.2 us)
Async XLA Ops:
  141.1 1.1 copy-start
  160.2 289.3 %all-to-all-start.1 = ((bf16[64,128,4,300]{1,2,3,0:T(4,128)(2,1)}), bf16[64,128,4,300]{1,2,3,0:T(4,128)(2,1)}, u32[]{:S(2)}, u32[]{:S(2)}) async-start(bf16[64,128,4,300]{1,2,3,0:T(4,128)(2,1)} %stack.2), calls=%async_computation.1 | async-start | bytes 39321600 | tf_op jit(solution)/shard_map/all_to_all | solution.py:50
  477.4 12.7 %collective-permute-start = (bf16[128,4,300]{0,2,1:T(8,128)(2,1)S(1)}, bf16[128,4,300]{0,2,1:T(8,128)(2,1)S(1)}, u32[]{:S(2)}, u32[]{:S(2)}) collective-permute-start(bf16[128,4,300]{0,2,1:T(8,128)(2,1)S(1)} %slice.62), channel_id=1, source_target_pairs={{0,1},{1,2},{2,3},{3,4},{4,5},{5,6},{6,7},{7,8},{8,9},{9,10},{10,1... | collective-permute-start | bytes 921608 | tf_op jit(solution)/shard_map/ppermute | solution.py:15
